TPU v7x, 256 devices: a whole 4x4x8 slice. The times are simulated.
256 devices in a mesh: dp: 4 (over x), tensor: 64 (over y, z, core).
Axes of the slice: x: 4, y: 4, z: 8, core: 2. Of those that a mesh axis runs over, the one named last changes fastest.
Arguments:
- tokens_in: bfloat16 [512, 4096], P('dp', 'tensor'), may hold values from -6 to 6
- out_grad: bfloat16 [512, 4096], P('dp', 'tensor'), may hold values from -6 to 6
- gate_blocks: bfloat16 [2048, 128, 128], P('tensor'), may hold values from -0.125 to 0.125
- up_blocks: bfloat16 [2048, 128, 128], P('tensor'), may hold values from -0.125 to 0.125
- down_blocks: bfloat16 [2048, 128, 128], P('tensor'), may hold values from -0.0625 to 0.0625
- gate_up_index: int32 [64, 32, 2], replicated, may hold values from 0 to 127, as said below
- down_index: int32 [64, 32, 2], replicated, may hold values from 0 to 127, as said below
Outputs:
- output: bfloat16 [512, 4096], P('dp', 'tensor')
- in_grad: bfloat16 [512, 4096], P('dp', 'tensor')
- gate_grads: bfloat16 [2048, 128, 128], P('tensor', 'dp')
- up_grads: bfloat16 [2048, 128, 128], P('tensor', 'dp')
- down_grads: bfloat16 [2048, 128, 128], P('tensor', 'dp')
Inputs may be any that keep to these rules, and one draw needn't show every extreme that they name: `gate_up_index`: Model-width blocks lie in 0 to 31, hidden-unit blocks in 0 to 127. No block is listed twice. The owner of hidden-unit block j is index j // 2 of tensor. Of one index's 32 entries at most 1 name hidden-unit blocks of any one owner, and in every draw some owner has exactly 1 entries from every index; other owners get from none up to all indices. `down_index`: Hidden-unit blocks lie in 0 to 127, model-width blocks in 0 to 31. No block is listed twice. The owner of hidden-unit block j is index j // 2 of tensor. Of one index's 32 entries at most 1 name hidden-unit blocks of any one owner, and in every draw some owner has exactly 1 entries from every index; other owners get from none up to all indices.
All inputs are finite; a program needn't handle non-finite values.
Results may differ from a plain program's by a relative error of at most 0.022.
Values may be sent and summed in bfloat16 or wider, within the bound.
A program may use at most 128 MiB of HBM per device.

v0:
```python
import jax
import jax.numpy as jnp
from jax import lax
from jax.sharding import PartitionSpec as P

FB = 128


def routing(index_list, key_col, other_col, own_count, slot_cap, my_index):
    tensor_size = index_list.shape[0]
    held_count = index_list.shape[1]
    key_blocks = index_list[:, :, key_col]
    other_idx = index_list[:, :, other_col]
    owners = key_blocks // own_count
    local_idx = key_blocks % own_count
    block_order = jnp.arange(held_count)
    before = block_order[None, :] < block_order[:, None]
    same_owner = owners[:, :, None] == owners[:, None, :]
    slot_rank = jnp.sum(jnp.logical_and(same_owner, before[None]), axis=2)
    slot_all = owners * slot_cap + slot_rank
    matches = jnp.logical_and(
        (owners == my_index)[:, :, None],
        slot_rank[:, :, None] == jnp.arange(slot_cap)[None, None, :],
    )
    is_found = jnp.any(matches, axis=1)
    recv_local = jnp.where(
        is_found, jnp.sum(jnp.where(matches, local_idx[:, :, None], 0), axis=1), -1
    )
    recv_other = jnp.sum(jnp.where(matches, other_idx[:, :, None], 0), axis=1)
    mine_slot = lax.dynamic_index_in_dim(slot_all, my_index, 0, keepdims=False)
    return (
        mine_slot,
        recv_local.reshape(tensor_size * slot_cap),
        recv_other.reshape(tensor_size * slot_cap),
    )


def per_device(tokens_in, out_grad, gate_blocks, up_blocks, down_blocks, gate_up_index, down_index):
    block_size = gate_blocks.shape[1]
    held_count = gate_blocks.shape[0]
    tok_rows = tokens_in.shape[0]
    tensor_size = lax.axis_size("tensor")
    my_index = lax.axis_index("tensor")
    blocks_f = FB
    own_count = blocks_f // tensor_size
    slot_cap = 2 * held_count // tensor_size
    slot_total = tensor_size * slot_cap
    gu_slot, gu_local, gu_other = routing(gate_up_index, 1, 0, own_count, slot_cap, my_index)
    dn_slot, dn_local, dn_other = routing(down_index, 0, 1, own_count, slot_cap, my_index)
    gu_mine = lax.dynamic_index_in_dim(gate_up_index, my_index, 0, keepdims=False)
    dn_mine = lax.dynamic_index_in_dim(down_index, my_index, 0, keepdims=False)
    own_ids = jnp.arange(own_count)[None, :]
    gu_onehot = (gu_local[:, None] == own_ids).astype(jnp.float32)
    dn_onehot = (dn_local[:, None] == own_ids).astype(jnp.float32)
    paired = jnp.concatenate([gate_blocks, up_blocks], axis=2)
    x_whole = lax.all_gather(tokens_in, "tensor", axis=1, tiled=True)
    blocks_d = x_whole.shape[1] // block_size
    x_blocks = x_whole.reshape(tok_rows, blocks_d, block_size)
    x_sel = jnp.take(x_blocks, gu_mine[:, 0], axis=1)
    partials = jnp.einsum("rnk,nkf->rnf", x_sel, paired, preferred_element_type=jnp.float32)
    outgoing = (
        jnp.zeros((tok_rows, slot_total, 2 * block_size), jnp.float32).at[:, gu_slot].set(partials)
    )
    arrived = lax.all_to_all(
        outgoing.astype(jnp.bfloat16), "tensor", split_axis=1, concat_axis=1, tiled=True
    ).astype(outgoing.dtype)
    col_sums = jnp.einsum("rsf,sl->rlf", arrived, gu_onehot, precision=lax.Precision.HIGHEST)
    gate_sum = col_sums[:, :, :block_size]
    up_sum = col_sums[:, :, block_size:]
    gate_sig = jax.nn.sigmoid(gate_sum)
    gate_act = gate_sum * gate_sig
    hidden = (gate_act * up_sum).astype(jnp.bfloat16)
    grad_whole = lax.all_gather(out_grad, "tensor", axis=1, tiled=True)
    grad_blocks = grad_whole.reshape(tok_rows, blocks_d, block_size)
    hidden_all = lax.all_gather(
        hidden.reshape(tok_rows, own_count * block_size), "tensor", axis=1, tiled=True
    )
    h_sel = jnp.take(hidden_all.reshape(tok_rows, blocks_f, block_size), dn_mine[:, 0], axis=1)
    out_parts = jnp.einsum("rnk,nkf->rnf", h_sel, down_blocks, preferred_element_type=jnp.float32)
    d_onehot = (dn_mine[:, 1][:, None] == jnp.arange(blocks_d)[None, :]).astype(jnp.float32)
    out_dense = jnp.einsum("rnf,nd->rdf", out_parts, d_onehot, precision=lax.Precision.HIGHEST)
    dy_sel = jnp.take(grad_blocks, dn_mine[:, 1], axis=1)
    hid_parts = jnp.einsum("rnf,nkf->rnk", dy_sel, down_blocks, preferred_element_type=jnp.float32)
    outgoing_h = (
        jnp.zeros((tok_rows, slot_total, block_size), jnp.float32).at[:, dn_slot].set(hid_parts)
    )
    arrived_dh = lax.all_to_all(
        outgoing_h.astype(jnp.bfloat16), "tensor", split_axis=1, concat_axis=1, tiled=True
    ).astype(outgoing_h.dtype)
    hidden_grad = jnp.einsum("rsf,sl->rlf", arrived_dh, dn_onehot, precision=lax.Precision.HIGHEST)
    down_w_grad = jnp.einsum("rnk,rnf->nkf", h_sel, dy_sel, preferred_element_type=jnp.float32)
    output = lax.psum_scatter(
        out_dense.reshape(tok_rows, blocks_d * block_size),
        "tensor",
        scatter_dimension=1,
        tiled=True,
    ).astype(jnp.bfloat16)
    gate_grad = hidden_grad * up_sum * gate_sig * (1.0 + gate_sum * (1.0 - gate_sig))
    up_grad = hidden_grad * gate_act
    both_grads = jnp.concatenate(
        [gate_grad.astype(jnp.bfloat16), up_grad.astype(jnp.bfloat16)], axis=2
    )
    back_send = jnp.take(both_grads, jnp.maximum(gu_local, 0), axis=1)
    back_send = jnp.where((gu_local >= 0)[None, :, None], back_send, jnp.zeros_like(back_send))
    returned = lax.all_to_all(back_send, "tensor", split_axis=1, concat_axis=1, tiled=True)
    gu_sel = jnp.take(returned, gu_slot, axis=1)
    gate_w_grad = jnp.einsum(
        "rnk,rnf->nkf", x_sel, gu_sel[:, :, :block_size], preferred_element_type=jnp.float32
    )
    up_w_grad = jnp.einsum(
        "rnk,rnf->nkf", x_sel, gu_sel[:, :, block_size:], preferred_element_type=jnp.float32
    )
    in_parts = jnp.einsum("rnf,nkf->rnk", gu_sel, paired, preferred_element_type=jnp.float32)
    r_onehot = (gu_mine[:, 0][:, None] == jnp.arange(blocks_d)[None, :]).astype(jnp.float32)
    in_dense = jnp.einsum("rnk,nd->rdk", in_parts, r_onehot, precision=lax.Precision.HIGHEST)
    in_grad = lax.psum_scatter(
        in_dense.reshape(tok_rows, blocks_d * block_size), "tensor", scatter_dimension=1, tiled=True
    ).astype(jnp.bfloat16)
    summed = (
        lax.psum_scatter(
            gate_w_grad.astype(jnp.bfloat16), "dp", scatter_dimension=1, tiled=True
        ).astype(jnp.float32),
        lax.psum_scatter(
            up_w_grad.astype(jnp.bfloat16), "dp", scatter_dimension=1, tiled=True
        ).astype(jnp.float32),
        lax.psum_scatter(
            down_w_grad.astype(jnp.bfloat16), "dp", scatter_dimension=1, tiled=True
        ).astype(jnp.float32),
    )
    return (
        output,
        in_grad,
        summed[0].astype(jnp.bfloat16),
        summed[1].astype(jnp.bfloat16),
        summed[2].astype(jnp.bfloat16),
    )


def solution(mesh):
    in_specs = (
        P("dp", "tensor"),
        P("dp", "tensor"),
        P("tensor", None, None),
        P("tensor", None, None),
        P("tensor", None, None),
        P(),
        P(),
    )
    out_specs = (
        P("dp", "tensor"),
        P("dp", "tensor"),
        P("tensor", "dp", None),
        P("tensor", "dp", None),
        P("tensor", "dp", None),
    )
    return jax.shard_map(
        per_device, mesh=mesh, in_specs=in_specs, out_specs=out_specs, check_vma=False
    )
```

profile of v0, /device:TPU:8, one launch (start us, length us, event | category | flops | bytes accessed | tf_op | source)
XLA Modules:
  0.0 843.3 jit_solution(729895510610050165)
XLA Ops:
  8.7 0.8 slice.31
  9.5 0.9 constant_dynamic-slice_fusion
  11.3 77.8 %all-gather.8.cloned.1.call-done = bf16[128,4096]{0,1:T(8,128)(2,1)} async-done(((bf16[128,64]{0,1:T(8,128)(2,1)}), bf16[128,4096]{0,1:T(8,128)(2,1)}) %all-gather.8.cloned.1.call-update) | async-done | bytes 1048592 | tf_op jit(solution)/shard_map/all_gather | solution.py:73
  89.1 1.6 copy.135
  90.7 1.7 gather_fusion.4
  92.4 2.1 fusion.12
  94.5 2.5 broadcast_in_dim.93
  97.0 5.4 scatter_fusion.1
  102.4 3.9 convert_element_type.53
  106.3 8.2 all-to-all-start.1
  115.3 1.4 constant_dynamic-update-slice_fusion.1
  116.8 1.5 constant_dynamic-update-slice_fusion
  118.3 79.2 %all-gather.4.cloned.1.call-done = bf16[128,4096]{0,1:T(8,128)(2,1)} async-done(((bf16[128,64]{0,1:T(8,128)(2,1)}), bf16[128,4096]{0,1:T(8,128)(2,1)}) %all-gather.4.cloned.1.call-update) | async-done | bytes 1048592 | tf_op jit(solution)/shard_map/all_gather | solution.py:56
  197.5 2.9 gather_fusion.3
  200.4 4.3 fusion.18
  204.8 4.2 broadcast_in_dim.88
  209.0 8.3 scatter_fusion
  217.3 6.0 convert_element_type.49
  223.3 8.2 all-to-all-start
  231.6 2.8 fusion.2
  234.5 91.9 %all-to-all-done = bf16[128,64,256]{2,0,1:T(8,128)(2,1)} async-done(((bf16[128,64,256]{2,0,1:T(8,128)(2,1)}), bf16[128,64,256]{2,0,1:T(8,128)(2,1)}, u32[]{:S(2)}, u32[]{:S(2)}) %all-to-all-start) | async-done | bytes 4194336 | tf_op jit(solution)/shard_map/all_to_all | solution.py:64
  326.3 4.5 fusion
  331.0 2.8 gather_fusion.1
  333.8 4.0 select_bitcast_fusion
  337.8 7.0 all-to-all-start.2
  345.7 106.2 %all-to-all-done.2 = bf16[128,64,256]{2,0,1:T(8,128)(2,1)} async-done(((bf16[128,64,256]{2,0,1:T(8,128)(2,1)}), bf16[128,64,256]{2,0,1:T(8,128)(2,1)}, u32[]{:S(2)}, u32[]{:S(2)}) %all-to-all-start.2) | async-done | bytes 4194336 | tf_op jit(solution)/shard_map/all_to_all | solution.py:105
  451.9 4.3 gather_fusion.2
  456.2 1.8 select_bitcast_fusion.1
  458.0 1.3 copy-done.1
  459.3 2.0 convolution_bitcast_fusion.1
  461.4 2.4 copy.138
  463.7 2.4 convolution_bitcast_fusion
  466.1 3.0 copy.144
  469.5 6.4 copy.131
  475.9 3.0 gather_fusion
  479.9 2.4 fusion.6
  482.3 1.9 copy.143
  484.3 1.5 copy-done.2
  485.8 2.7 convolution_convert_fusion.2
  488.6 2.7 convolution_convert_fusion.1
  491.4 3.2 convolution_convert_fusion
  494.6 112.1 %reduce-scatter.8.cloned.1.call-done = f32[128,64]{0,1:T(8,128)} async-done(((f32[128,4096]{0,1:T(8,128)}), f32[128,64]{0,1:T(8,128)}) %reduce-scatter.8.cloned.1.call-update) | async-done | bytes 32784 | tf_op jit(solution)/shard_map/reduce_scatter | solution.py:116
  606.7 1.4 convert_element_type.56
  608.1 142.1 %reduce-scatter.6.cloned.1.call-done = f32[128,64]{0,1:T(8,128)} async-done(((f32[128,4096]{0,1:T(8,128)}), f32[128,64]{0,1:T(8,128)}) %reduce-scatter.6.cloned.1.call-update) | async-done | bytes 32784 | tf_op jit(solution)/shard_map/reduce_scatter | solution.py:92
  750.2 1.4 convert_element_type.51
  751.5 26.8 %reduce-scatter.10.cloned.1.call-done = bf16[32,32,128]{2,1,0:T(8,128)(2,1)} async-done(((bf16[32,128,128]{2,1,0:T(8,128)(2,1)}), bf16[32,32,128]{2,1,0:T(8,128)(2,1)}) %reduce-scatter.10.cloned.1.call-update) | async-done | bytes 262160 | tf_op jit(solution)/shard_map/reduce_scatter | solution.py:120
  778.4 29.1 %reduce-scatter.12.cloned.1.call-done = bf16[32,32,128]{2,1,0:T(8,128)(2,1)} async-done(((bf16[32,128,128]{2,1,0:T(8,128)(2,1)}), bf16[32,32,128]{2,1,0:T(8,128)(2,1)}) %reduce-scatter.12.cloned.1.call-update) | async-done | bytes 262160 | tf_op jit(solution)/shard_map/reduce_scatter | solution.py:123
  807.5 29.0 %reduce-scatter.14.cloned.1.call-done = bf16[32,32,128]{2,1,0:T(8,128)(2,1)} async-done(((bf16[32,128,128]{2,1,0:T(8,128)(2,1)}), bf16[32,32,128]{2,1,0:T(8,128)(2,1)}) %reduce-scatter.14.cloned.1.call-update) | async-done | bytes 262160 | tf_op jit(solution)/shard_map/reduce_scatter | solution.py:126
  (59 shorter events, 5.8 us)
Async XLA Ops:
  7.2 85.3 %copy-start = (bf16[32,128,128]{2,1,0:T(8,128)(2,1)S(1)}, bf16[32,128,128]{2,1,0:T(8,128)(2,1)}, u32[]{:S(2)}) copy-start(bf16[32,128,128]{2,1,0:T(8,128)(2,1)} %param.13) | copy-start | bytes 3145732
  7.2 81.9 %all-gather.8.cloned.1.call-start = ((), (), s32[]{:S(2)}) async-start(), calls=%async_computation.11 | async-start | bytes 1064960 | tf_op jit(solution)/shard_map/all_gather | solution.py:73
  106.3 117.0 %all-to-all-start.1 = ((bf16[128,64,128]{2,0,1:T(8,128)(2,1)}), bf16[128,64,128]{2,0,1:T(8,128)(2,1)}, u32[]{:S(2)}, u32[]{:S(2)}) async-start(bf16[128,64,128]{2,0,1:T(8,128)(2,1)} %convert_element_type.53), calls=%async_computation.2 | async-start | bytes 4194304 | tf_op jit(solution)/shard_map/all_to_all | solution.py:87
  114.5 83.0 %all-gather.4.cloned.1.call-start = ((), (), s32[]{:S(2)}) async-start(), calls=%async_computation.8 | async-start | bytes 1064960 | tf_op jit(solution)/shard_map/all_gather | solution.py:56
  223.3 103.0 %all-to-all-start = ((bf16[128,64,256]{2,0,1:T(8,128)(2,1)}), bf16[128,64,256]{2,0,1:T(8,128)(2,1)}, u32[]{:S(2)}, u32[]{:S(2)}) async-start(bf16[128,64,256]{2,0,1:T(8,128)(2,1)} %convert_element_type.49), calls=%async_computation | async-start | bytes 8388608 | tf_op jit(solution)/shard_map/all_to_all | solution.py:64
  337.8 114.1 %all-to-all-start.2 = ((bf16[128,64,256]{2,0,1:T(8,128)(2,1)}), bf16[128,64,256]{2,0,1:T(8,128)(2,1)}, u32[]{:S(2)}, u32[]{:S(2)}) async-start(bf16[128,64,256]{2,0,1:T(8,128)(2,1)} %select_bitcast_fusion), calls=%async_computation.3 | async-start | bytes 8388608 | tf_op jit(solution)/shard_map/all_to_all | solution.py:105
  344.7 124.8 %all-gather.6.cloned.1.call-start = ((), (), s32[]{:S(2)}) async-start(), calls=%async_computation.9 | async-start | bytes 4259840 | tf_op jit(solution)/shard_map/all_gather | solution.py:75
  345.6 261.1 %reduce-scatter.8.cloned.1.call-start = ((), (), s32[]{:S(2)}) async-start(), calls=%async_computation.12 | async-start | bytes 2129920 | tf_op jit(solution)/shard_map/reduce_scatter | solution.py:116
  458.0 1.3 copy-start.1
  469.2 281.0 %reduce-scatter.6.cloned.1.call-start = ((), (), s32[]{:S(2)}) async-start(), calls=%async_computation.10 | async-start | bytes 2129920 | tf_op jit(solution)/shard_map/reduce_scatter | solution.py:92
  478.9 1.0 copy-start.3
  484.2 1.6 copy-start.2
  484.2 294.1 %reduce-scatter.10.cloned.1.call-start = ((), (), s32[]{:S(2)}) async-start(), calls=%async_computation.13 | async-start | bytes 1310720 | tf_op jit(solution)/shard_map/reduce_scatter | solution.py:120
  488.6 318.9 %reduce-scatter.12.cloned.1.call-start = ((), (), s32[]{:S(2)}) async-start(), calls=%async_computation.14 | async-start | bytes 1310720 | tf_op jit(solution)/shard_map/reduce_scatter | solution.py:123
  491.4 345.1 %reduce-scatter.14.cloned.1.call-start = ((), (), s32[]{:S(2)}) async-start(), calls=%async_computation.15 | async-start | bytes 1310720 | tf_op jit(solution)/shard_map/reduce_scatter | solution.py:126
Sparse Core Ops, SparseCore 0:
  10.8 78.2 all-gather.7
  118.1 79.3 all-gather.3
  348.9 99.5 all-gather.5
  469.3 137.3 reduce-scatter.7
  611.2 138.9 reduce-scatter.5
  753.1 25.1 reduce-scatter.9
  781.6 25.8 reduce-scatter.11
  810.6 25.8 reduce-scatter.13
where the time goes:
time: 845 us; the launch traced here: 843 us
  waiting for transfers between devices  696 us (82%)
  local copies, waits for them, and re-layouts  60 us (7%)
  matrix products  29.7 us (4%)
  starting transfers between devices  23.9 us (3%)
  other arithmetic  19.5 us (2%)
  between operations  14.4 us (2%)
    reduce_scatter x1, waiting for transfers between devices, per_device(): lax.psum_scatter(out_dense.reshape(tok_rows, blocks_d * block_size), 'ten...  142 us
    reduce_scatter x1, waiting for transfers between devices, per_device(): lax.psum_scatter(in_dense.reshape(tok_rows, blocks_d * block_size), 'tens...  112 us
    all_to_all x1, waiting for transfers between devices, per_device(): lax.all_to_all(back_send, 'tensor', split_axis=1, concat_axis=1, tiled=True)  106 us
    all_to_all x1, waiting for transfers between devices, per_device(): lax.all_to_all(outgoing.astype(jnp.bfloat16), 'tensor', split_axis=1, con...  91.9 us
    all_gather x1, waiting for transfers between devices, per_device(): x_whole = lax.all_gather(tokens_in, 'tensor', axis=1, tiled=True)  79.2 us
    all_gather x1, waiting for transfers between devices, per_device(): grad_whole = lax.all_gather(out_grad, 'tensor', axis=1, tiled=True)  77.8 us
    reduce_scatter x1, waiting for transfers between devices, per_device(): lax.psum_scatter(up_w_grad.astype(jnp.bfloat16), 'dp', scatter_dimension=...  29.1 us
    reduce_scatter x1, waiting for transfers between devices, per_device(): lax.psum_scatter(down_w_grad.astype(jnp.bfloat16), 'dp', scatter_dimensio...  29 us
  transfers between devices with their start and end apart: 11, of which 9 were waited for; matrix products, arithmetic and copies ran while one was open for 9% of the time, Pallas kernels for 0%

commit v1 on v0

--- a/solution.py
+++ b/solution.py
@@ -53,7 +53,9 @@
     gu_onehot = (gu_local[:, None] == own_ids).astype(jnp.float32)
     dn_onehot = (dn_local[:, None] == own_ids).astype(jnp.float32)
     paired = jnp.concatenate([gate_blocks, up_blocks], axis=2)
-    x_whole = lax.all_gather(tokens_in, "tensor", axis=1, tiled=True)
+    x_whole = jnp.concatenate(
+        lax.all_to_all(jnp.stack([tokens_in] * lax.axis_size("tensor")), "tensor", 0, 0), axis=1
+    )
     blocks_d = x_whole.shape[1] // block_size
     x_blocks = x_whole.reshape(tok_rows, blocks_d, block_size)
     x_sel = jnp.take(x_blocks, gu_mine[:, 0], axis=1)

time: 845 us -> 787 us (0.931)
  waiting for transfers between devices: 696 us -> 624 us
  starting transfers between devices: 23.9 us -> 35.6 us
    all_gather x1 -> x0, waiting for transfers between devices: 79.2 us -> none  [per_device(): x_whole = lax.all_gather(tokens_in, 'tensor', axis=1, tiled=True)]
    all_to_all x1, waiting for transfers between devices: 0.01 us -> 18.8 us  [per_device(): lax.all_to_all(outgoing_h.astype(jnp.bfloat16), 'tensor', split_axis=1, c...]
    all_to_all x0 -> x1, starting transfers between devices: none -> 12.3 us  [per_device(): lax.all_to_all(jnp.stack([tokens_in] * lax.axis_size('tensor')), 'tensor'...]
    all_gather x1, waiting for transfers between devices: 77.8 us -> 67.6 us  [per_device(): grad_whole = lax.all_gather(out_grad, 'tensor', axis=1, tiled=True)]
  transfers between devices with their start and end apart: 11 -> 11, of which waited for: 9 -> 9; matrix products, arithmetic and copies ran while one was open for 9% -> 12% of each run, Pallas kernels for 0% -> 0%
where the time goes in v1:
time: 787 us; the launch traced here: 785 us
  waiting for transfers between devices  624 us (79%)
  local copies, waits for them, and re-layouts  61.8 us (8%)
  starting transfers between devices  35.6 us (5%)
  matrix products  29.5 us (4%)
  other arithmetic  19.3 us (2%)
  between operations  14.5 us (2%)
    reduce_scatter x1, waiting for transfers between devices, per_device(): lax.psum_scatter(out_dense.reshape(tok_rows, blocks_d * block_size), 'ten...  142 us
    reduce_scatter x1, waiting for transfers between devices, per_device(): lax.psum_scatter(in_dense.reshape(tok_rows, blocks_d * block_size), 'tens...  112 us
    all_to_all x1, waiting for transfers between devices, per_device(): lax.all_to_all(back_send, 'tensor', split_axis=1, concat_axis=1, tiled=True)  106 us
    all_to_all x1, waiting for transfers between devices, per_device(): lax.all_to_all(outgoing.astype(jnp.bfloat16), 'tensor', split_axis=1, con...  91.9 us
    all_gather x1, waiting for transfers between devices, per_device(): grad_whole = lax.all_gather(out_grad, 'tensor', axis=1, tiled=True)  67.6 us
    reduce_scatter x1, waiting for transfers between devices, per_device(): lax.psum_scatter(up_w_grad.astype(jnp.bfloat16), 'dp', scatter_dimension=...  29 us
    reduce_scatter x1, waiting for transfers between devices, per_device(): lax.psum_scatter(down_w_grad.astype(jnp.bfloat16), 'dp', scatter_dimensio...  29 us
    reduce_scatter x1, waiting for transfers between devices, per_device(): lax.psum_scatter(gate_w_grad.astype(jnp.bfloat16), 'dp', scatter_dimensio...  26.8 us
  transfers between devices with their start and end apart: 11, of which 9 were waited for; matrix products, arithmetic and copies ran while one was open for 12% of the time, Pallas kernels for 0%

profile of v1, /device:TPU:8, one launch (start us, length us, event | category | flops | bytes accessed | tf_op | source)
XLA Modules:
  0.0 785.1 jit_solution(705515270030132752)
XLA Ops:
  7.9 2.0 stack.2
  9.9 12.3 %all-to-all-start = ((bf16[64,128,64]{1,2,0:T(8,128)(2,1)}), bf16[64,128,64]{1,2,0:T(8,128)(2,1)}, u32[]{:S(2)}, u32[]{:S(2)}) async-start(bf16[64,128,64]{1,2,0:T(8,128)(2,1)} %stack.2), calls=%async_computation | async-start | bytes 2097152 | tf_op jit(solution)/shard_map/all_to_all | solution.py:57
  23.2 67.6 %all-gather.5.cloned.1.call-done = bf16[128,4096]{0,1:T(8,128)(2,1)} async-done(((bf16[128,64]{0,1:T(8,128)(2,1)}), bf16[128,4096]{0,1:T(8,128)(2,1)}) %all-gather.5.cloned.1.call-update) | async-done | bytes 1048592 | tf_op jit(solution)/shard_map/all_gather | solution.py:75
  90.8 1.6 copy.147
  92.4 1.7 gather_fusion.4
  94.1 2.1 fusion.12
  96.2 2.4 broadcast_in_dim.93
  98.7 5.4 scatter_fusion.1
  104.0 3.9 convert_element_type.53
  107.9 8.2 %all-to-all-start.2 = ((bf16[128,64,128]{2,0,1:T(8,128)(2,1)}), bf16[128,64,128]{2,0,1:T(8,128)(2,1)}, u32[]{:S(2)}, u32[]{:S(2)}) async-start(bf16[128,64,128]{2,0,1:T(8,128)(2,1)} %convert_element_type.53), calls=%async_computation.3 | async-start | bytes 4194304 | tf_op jit(solution)/shard_map/all_to_all | solution.py:89
  116.2 1.4 constant_dynamic-update-slice_fusion.1
  117.6 1.5 constant_dynamic-update-slice_fusion
  119.2 2.3 copy.139
  121.4 2.9 gather_fusion.3
  124.4 3.9 fusion.18
  128.3 4.2 broadcast_in_dim.88
  132.5 8.3 %scatter_fusion = f32[128,64,256]{2,0,1:T(8,128)} fusion(f32[128,64,256]{2,0,1:T(8,128)} %broadcast_in_dim.88, s32[32]{0:T(128)S(1)} %fusion.51, f32[32,128,256]{2,1,0:T(8,128)} %fusion.18), kind=kCustom, calls=%fused_computation.5 | custom fusion | bytes 12583040 | tf_op jit(solution)/shard_map/scatter | solution.py:64
  140.8 6.0 convert_element_type.49
  146.8 18.8 %all-to-all-done.2 = bf16[128,64,128]{2,0,1:T(8,128)(2,1)} async-done(((bf16[128,64,128]{2,0,1:T(8,128)(2,1)}), bf16[128,64,128]{2,0,1:T(8,128)(2,1)}, u32[]{:S(2)}, u32[]{:S(2)}) %all-to-all-start.2) | async-done | bytes 2097184 | tf_op jit(solution)/shard_map/all_to_all | solution.py:89
  165.6 7.7 all-to-all-start.1
  173.5 2.8 fusion.2
  176.3 91.9 %all-to-all-done.1 = bf16[128,64,256]{2,0,1:T(8,128)(2,1)} async-done(((bf16[128,64,256]{2,0,1:T(8,128)(2,1)}), bf16[128,64,256]{2,0,1:T(8,128)(2,1)}, u32[]{:S(2)}, u32[]{:S(2)}) %all-to-all-start.1) | async-done | bytes 4194336 | tf_op jit(solution)/shard_map/all_to_all | solution.py:66
  268.1 4.5 fusion
  272.8 2.8 gather_fusion.1
  275.6 4.0 select_bitcast_fusion
  279.6 7.0 all-to-all-start.3
  287.4 106.2 %all-to-all-done.3 = bf16[128,64,256]{2,0,1:T(8,128)(2,1)} async-done(((bf16[128,64,256]{2,0,1:T(8,128)(2,1)}), bf16[128,64,256]{2,0,1:T(8,128)(2,1)}, u32[]{:S(2)}, u32[]{:S(2)}) %all-to-all-start.3) | async-done | bytes 4194336 | tf_op jit(solution)/shard_map/all_to_all | solution.py:107
  393.7 4.2 gather_fusion.2
  397.9 1.8 select_bitcast_fusion.1
  401.1 2.0 convolution_bitcast_fusion.1
  403.1 2.4 copy.150
  405.5 2.4 convolution_bitcast_fusion
  407.9 3.0 copy.159
  411.2 6.4 copy.143
  417.6 3.0 gather_fusion
  421.6 2.4 fusion.6
  424.0 1.9 copy.158
  426.0 1.5 copy-done.2
  427.5 2.8 convolution_convert_fusion.2
  430.4 2.8 convolution_convert_fusion.1
  433.3 3.2 convolution_convert_fusion
  436.5 112.0 %reduce-scatter.8.cloned.1.call-done = f32[128,64]{0,1:T(8,128)} async-done(((f32[128,4096]{0,1:T(8,128)}), f32[128,64]{0,1:T(8,128)}) %reduce-scatter.8.cloned.1.call-update) | async-done | bytes 32784 | tf_op jit(solution)/shard_map/reduce_scatter | solution.py:118
  548.5 1.4 convert_element_type.56
  549.8 142.2 %reduce-scatter.6.cloned.1.call-done = f32[128,64]{0,1:T(8,128)} async-done(((f32[128,4096]{0,1:T(8,128)}), f32[128,64]{0,1:T(8,128)}) %reduce-scatter.6.cloned.1.call-update) | async-done | bytes 32784 | tf_op jit(solution)/shard_map/reduce_scatter | solution.py:94
  692.0 1.4 convert_element_type.51
  693.4 26.8 %reduce-scatter.10.cloned.1.call-done = bf16[32,32,128]{2,1,0:T(8,128)(2,1)} async-done(((bf16[32,128,128]{2,1,0:T(8,128)(2,1)}), bf16[32,32,128]{2,1,0:T(8,128)(2,1)}) %reduce-scatter.10.cloned.1.call-update) | async-done | bytes 262160 | tf_op jit(solution)/shard_map/reduce_scatter | solution.py:122
  720.3 29.0 %reduce-scatter.12.cloned.1.call-done = bf16[32,32,128]{2,1,0:T(8,128)(2,1)} async-done(((bf16[32,128,128]{2,1,0:T(8,128)(2,1)}), bf16[32,32,128]{2,1,0:T(8,128)(2,1)}) %reduce-scatter.12.cloned.1.call-update) | async-done | bytes 262160 | tf_op jit(solution)/shard_map/reduce_scatter | solution.py:125
  749.2 29.0 %reduce-scatter.14.cloned.1.call-done = bf16[32,32,128]{2,1,0:T(8,128)(2,1)} async-done(((bf16[32,128,128]{2,1,0:T(8,128)(2,1)}), bf16[32,32,128]{2,1,0:T(8,128)(2,1)}) %reduce-scatter.14.cloned.1.call-update) | async-done | bytes 262160 | tf_op jit(solution)/shard_map/reduce_scatter | solution.py:128
  (64 shorter events, 5.6 us)
Async XLA Ops:
  7.2 86.9 %copy-start = (bf16[32,128,128]{2,1,0:T(8,128)(2,1)S(1)}, bf16[32,128,128]{2,1,0:T(8,128)(2,1)}, u32[]{:S(2)}) copy-start(bf16[32,128,128]{2,1,0:T(8,128)(2,1)} %param.13) | copy-start | bytes 3145732
  7.2 15.0 %copy-start.4 = (s32[64,32,2]{0,2,1:T(2,128)S(1)}, s32[64,32,2]{0,2,1:T(2,128)}, u32[]{:S(2)}) copy-start(s32[64,32,2]{0,2,1:T(2,128)} %param.15) | copy-start | bytes 49156
  7.2 15.0 %copy-start.5 = (s32[64,32,2]{0,2,1:T(2,128)S(1)}, s32[64,32,2]{0,2,1:T(2,128)}, u32[]{:S(2)}) copy-start(s32[64,32,2]{0,2,1:T(2,128)} %param.14) | copy-start | bytes 49156
  7.2 83.6 %all-gather.5.cloned.1.call-start = ((), (), s32[]{:S(2)}) async-start(), calls=%async_computation.11 | async-start | bytes 1064960 | tf_op jit(solution)/shard_map/all_gather | solution.py:75
  9.9 98.0 %all-to-all-start = ((bf16[64,128,64]{1,2,0:T(8,128)(2,1)}), bf16[64,128,64]{1,2,0:T(8,128)(2,1)}, u32[]{:S(2)}, u32[]{:S(2)}) async-start(bf16[64,128,64]{1,2,0:T(8,128)(2,1)} %stack.2), calls=%async_computation | async-start | bytes 2097152 | tf_op jit(solution)/shard_map/all_to_all | solution.py:57
  107.9 57.6 %all-to-all-start.2 = ((bf16[128,64,128]{2,0,1:T(8,128)(2,1)}), bf16[128,64,128]{2,0,1:T(8,128)(2,1)}, u32[]{:S(2)}, u32[]{:S(2)}) async-start(bf16[128,64,128]{2,0,1:T(8,128)(2,1)} %convert_element_type.53), calls=%async_computation.3 | async-start | bytes 4194304 | tf_op jit(solution)/shard_map/all_to_all | solution.py:89
  165.6 102.6 %all-to-all-start.1 = ((bf16[128,64,256]{2,0,1:T(8,128)(2,1)}), bf16[128,64,256]{2,0,1:T(8,128)(2,1)}, u32[]{:S(2)}, u32[]{:S(2)}) async-start(bf16[128,64,256]{2,0,1:T(8,128)(2,1)} %convert_element_type.49), calls=%async_computation.1 | async-start | bytes 8388608 | tf_op jit(solution)/shard_map/all_to_all | solution.py:66
  279.6 114.1 %all-to-all-start.3 = ((bf16[128,64,256]{2,0,1:T(8,128)(2,1)}), bf16[128,64,256]{2,0,1:T(8,128)(2,1)}, u32[]{:S(2)}, u32[]{:S(2)}) async-start(bf16[128,64,256]{2,0,1:T(8,128)(2,1)} %select_bitcast_fusion), calls=%async_computation.4 | async-start | bytes 8388608 | tf_op jit(solution)/shard_map/all_to_all | solution.py:107
  286.5 124.7 %all-gather.3.cloned.1.call-start = ((), (), s32[]{:S(2)}) async-start(), calls=%async_computation.9 | async-start | bytes 4259840 | tf_op jit(solution)/shard_map/all_gather | solution.py:77
  287.3 261.1 %reduce-scatter.8.cloned.1.call-start = ((), (), s32[]{:S(2)}) async-start(), calls=%async_computation.12 | async-start | bytes 2129920 | tf_op jit(solution)/shard_map/reduce_scatter | solution.py:118
  399.8 1.3 copy-start.1
  410.9 281.1 %reduce-scatter.6.cloned.1.call-start = ((), (), s32[]{:S(2)}) async-start(), calls=%async_computation.10 | async-start | bytes 2129920 | tf_op jit(solution)/shard_map/reduce_scatter | solution.py:94
  420.6 1.0 copy-start.3
  425.9 1.6 copy-start.2
  425.9 294.3 %reduce-scatter.10.cloned.1.call-start = ((), (), s32[]{:S(2)}) async-start(), calls=%async_computation.13 | async-start | bytes 1310720 | tf_op jit(solution)/shard_map/reduce_scatter | solution.py:122
  430.4 318.9 %reduce-scatter.12.cloned.1.call-start = ((), (), s32[]{:S(2)}) async-start(), calls=%async_computation.14 | async-start | bytes 1310720 | tf_op jit(solution)/shard_map/reduce_scatter | solution.py:125
  433.2 345.0 %reduce-scatter.14.cloned.1.call-start = ((), (), s32[]{:S(2)}) async-start(), calls=%async_computation.15 | async-start | bytes 1310720 | tf_op jit(solution)/shard_map/reduce_scatter | solution.py:128
Sparse Core Ops, SparseCore 0:
  10.8 79.9 all-gather.4
  290.7 98.8 all-gather.2
  411.0 137.4 reduce-scatter.7
  552.9 139.0 reduce-scatter.5
  695.0 25.1 reduce-scatter.9
  723.4 25.8 reduce-scatter.11
  752.4 25.8 reduce-scatter.13
